TPU v7x, 512 devices: a whole 4x8x8 slice. The times are simulated.
512 devices in a mesh: leaf: 128 (over z, y, core), sep: 4 (over x).
Axes of the slice: x: 4, y: 8, z: 8, core: 2. Of those that a mesh axis runs over, the one named last changes fastest.
Arguments:
- leaf_source: float32 [128, 640, 256], P('leaf', 'sep'), may hold values from -6 to 6
- leaf_inverse: float32 [128, 640, 640], P('leaf', 'sep'), as said below
- leaf_update: float32 [128, 896, 640], P('leaf', None, 'sep'), as said below
- row_lists: int32 [128, 896], P('leaf'), may hold values from 0 to 255
- row_counts: int32 [128, 7], P('leaf'), may hold values from 1 to 128, as said below
- separator_source: float32 [128, 256, 256], P('leaf', 'sep'), may hold values from -6 to 6
- separator_inverse: float32 [128, 256, 256], P('leaf'), as said below
- separator_coupling: float32 [128, 256, 256], P('leaf'), may hold values from -0.1875 to 0.1875
Outputs:
- leaf_solution: float32 [128, 640, 256], P('leaf', 'sep')
- separator_solution: float32 [128, 256, 256], P('leaf', 'sep')
Inputs may be any that keep to these rules, and one draw needn't show every extreme that they name: `leaf_inverse`: each leaf's block is lower triangular, zero above the diagonal, with diagonal entries between 0.6 and 1.4. `separator_inverse`: each block is lower triangular, zero above the diagonal, with diagonal entries between 0.6 and 1.4. `leaf_update`: row r of a leaf's block belongs to the leaf's ancestor of level 1 + r // 128. `row_lists`: entry r names a row of the leaf's ancestor of level 1 + r // 128. `row_counts`: at every level some leaf has 128 live rows.
All inputs are finite; a program needn't handle non-finite values.
Results may differ from a plain program's by a relative error of at most 0.00011.
Values sent between devices are 32-bit elements; how exact they have to be, the bound alone decides.
A program may use at most 64 MiB of HBM per device.

v0:
```python
import jax
import jax.numpy as jnp
from jax import lax
from jax.sharding import PartitionSpec as P

highest = lax.Precision.HIGHEST


def passed_along(x, axis, by):
    peers = lax.axis_size(axis)
    pairs = [(i, i + by) for i in range(peers) if 0 <= i + by < peers]
    return lax.ppermute(x, axis, pairs)


def product(matrix, operand):
    return jnp.dot(matrix, operand, precision=highest, preferred_element_type=jnp.float32)


def product_first(matrix, operand):
    return lax.dot_general(
        matrix,
        operand,
        (((0,), (0,)), ((), ())),
        precision=highest,
        preferred_element_type=jnp.float32,
    )


def tree_pass(payload, offset):
    return passed_along(payload, "leaf", offset)


def sep_rows(payload):
    return lax.all_gather(payload, "sep", axis=0, tiled=True)


def per_device(
    leaf_source,
    leaf_inverse,
    leaf_update,
    row_lists,
    row_counts,
    separator_source,
    separator_inverse,
    separator_coupling,
):
    depth = row_counts.shape[1]
    leaf_index = lax.axis_index("leaf")
    sep_index = lax.axis_index("sep")
    source = leaf_source[0]
    inverse = leaf_inverse[0]
    update = leaf_update[0]
    quarter = separator_source.shape[1]
    full_rows = separator_inverse.shape[1]
    columns = source.shape[1]
    capacity = row_lists.shape[1] // depth
    first_row = sep_index * quarter
    inverse_block = inverse
    leaf_y = product(inverse_block, lax.all_gather(source, "sep", axis=0, tiled=True))
    slot_index = jnp.arange(depth * capacity) % capacity
    limits = jnp.repeat(row_counts[0], capacity)
    live_rows = (slot_index < limits)[:, None]
    update_terms = jnp.where(live_rows, product(update, leaf_y), 0.0)
    targets = row_lists[0].reshape(depth, capacity)
    picker = (jnp.arange(full_rows)[None, :, None] == targets[:, None, :]).astype(jnp.float32)
    densified = jnp.einsum(
        "kwp,kpn->wkn",
        picker,
        update_terms.reshape(depth, capacity, columns),
        precision=highest,
        preferred_element_type=jnp.float32,
    )
    carried = lax.psum_scatter(densified, "sep", scatter_dimension=0, tiled=True)
    own_source = separator_source[0]
    solver_block = separator_inverse[0]
    coupling = separator_coupling[0]
    coupling_rows = lax.dynamic_slice_in_dim(coupling, first_row, quarter, 0)
    solved_down = jnp.zeros((full_rows, columns), jnp.float32)
    for height in range(1, depth + 1):
        upper_slots = carried[:, height - 1 :]
        stride = 2 ** max(height - 2, 0)
        from_left = tree_pass(upper_slots, stride)
        if height == 1:
            from_right = upper_slots
        else:
            from_right = tree_pass(upper_slots, -stride)
        is_owner = leaf_index % 2**height == 2 ** (height - 1)
        carried = carried.at[:, height - 1 :].set(
            jnp.where(is_owner, from_left + from_right, upper_slots)
        )
        residual_full = sep_rows(own_source - carried[:, height - 1])
        solved = product(solver_block, residual_full)
        solved_down = jnp.where(is_owner, solved, solved_down)
        if height < depth:
            carried = carried.at[:, height].add(
                jnp.where(is_owner, product(coupling_rows, solved), 0.0)
            )
    stacked = jnp.zeros(carried.shape, jnp.float32)
    solution_full = jnp.zeros((full_rows, columns), jnp.float32)
    for height in range(depth, 0, -1):
        is_owner = leaf_index % 2**height == 2 ** (height - 1)
        target = solved_down
        if height < depth:
            stride = 2 ** (height - 1)
            upper_slots = stacked[:, height:]
            from_below = tree_pass(upper_slots, stride)
            from_above = tree_pass(upper_slots, -stride)
            right_child = leaf_index // 2**height % 2 == 1
            received = jnp.where(right_child, from_below, from_above)
            stacked = stacked.at[:, height:].set(jnp.where(is_owner, received, upper_slots))
            parent_full = sep_rows(received[:, 0])
            target = solved_down - product_first(coupling, parent_full)
        solution = product_first(solver_block, target)
        solution_full = jnp.where(is_owner, solution, solution_full)
        own_rows = lax.dynamic_slice_in_dim(solution, first_row, quarter, 0)
        stacked = stacked.at[:, height - 1].set(
            jnp.where(is_owner, own_rows, stacked[:, height - 1])
        )
    from_next = tree_pass(stacked, -1)
    ancestors = jnp.where(leaf_index % 2 == 1, stacked, from_next)
    ancestors_full = sep_rows(ancestors)
    picked = jnp.einsum(
        "kwp,wkn->kpn",
        picker,
        ancestors_full,
        precision=highest,
        preferred_element_type=jnp.float32,
    )
    picked = jnp.where(live_rows, picked.reshape(depth * capacity, columns), 0.0)
    leaf_w = leaf_y - product_first(update, picked)
    inverse_block = inverse
    leaf_x = lax.psum_scatter(
        product_first(inverse_block, leaf_w), "sep", scatter_dimension=0, tiled=True
    )
    separator_rows = lax.dynamic_slice_in_dim(solution_full, first_row, quarter, 0)
    return (leaf_x[None], separator_rows[None])


def solution(mesh):
    placed = (
        P("leaf", "sep", None),
        P("leaf", "sep", None),
        P("leaf", None, "sep"),
        P("leaf", None),
        P("leaf", None),
        P("leaf", "sep", None),
        P("leaf", None, None),
        P("leaf", None, None),
    )
    return jax.shard_map(
        per_device,
        mesh=mesh,
        in_specs=placed,
        out_specs=(P("leaf", "sep", None), P("leaf", "sep", None)),
        check_vma=False,
    )
```

profile of v0, /device:TPU:8, one launch (start us, length us, event | category | flops | bytes accessed | tf_op | source)
XLA Modules:
  0.0 518.3 jit_solution(3606953752508697259)
XLA Ops:
  7.2 13.7 %all-gather = f32[1,640,256]{2,1,0:T(8,128)S(1)} all-gather(f32[1,160,256]{2,1,0:T(8,128)} %param.62), channel_id=2, replica_groups=mesh['leaf'=128,'sep'=4] {'sep'}, dimensions={1}, use_global_device_ids=true | all-gather | bytes 819200 | tf_op jit(solution)/shard_map/all_gather | solution.py:59
  27.9 39.7 %reduce-scatter.5.cloned.1.call-done = f32[64,7,256]{2,1,0:T(8,128)} async-done(((f32[256,7,256]{2,1,0:T(8,128)}), f32[64,7,256]{2,1,0:T(8,128)}) %reduce-scatter.5.cloned.1.call-update) | async-done | bytes 458768 | tf_op jit(solution)/shard_map/reduce_scatter | solution.py:73
  70.7 7.9 %collective-permute-done = f32[64,7,256]{2,0,1:T(8,128)S(1)} collective-permute-done((f32[64,7,256]{2,0,1:T(8,128)S(1)}, f32[64,7,256]{2,0,1:T(8,128)S(1)}, u32[]{:S(2)}, u32[]{:S(2)}) %collective-permute-start) | collective-permute-done | bytes 458784 | tf_op jit(solution)/shard_map/ppermute | solution.py:12
  79.8 12.4 %all_gather.46 = f32[256,256]{1,0:T(8,128)S(1)} all-gather(f32[64,256]{1,0:T(8,128)S(1)} %fusion.94), channel_id=1, replica_groups=mesh['leaf'=128,'sep'=4] {'sep'}, dimensions={0}, use_global_device_ids=true | all-gather | bytes 327680 | tf_op jit(solution)/shard_map/all_gather | solution.py:34
  104.2 12.5 %all_gather.47 = f32[256,256]{1,0:T(8,128)S(1)} all-gather(f32[64,256]{1,0:T(8,128)S(1)} %fusion.92), channel_id=1, replica_groups=mesh['leaf'=128,'sep'=4] {'sep'}, dimensions={0}, use_global_device_ids=true | all-gather | bytes 327680 | tf_op jit(solution)/shard_map/all_gather | solution.py:34
  133.2 12.3 %all_gather.48 = f32[256,256]{1,0:T(8,128)S(1)} all-gather(f32[64,256]{1,0:T(8,128)S(1)} %fusion.90), channel_id=1, replica_groups=mesh['leaf'=128,'sep'=4] {'sep'}, dimensions={0}, use_global_device_ids=true | all-gather | bytes 327680 | tf_op jit(solution)/shard_map/all_gather | solution.py:34
  146.5 6.2 %collective-permute-start.5 = (f32[64,4,256]{2,0,1:T(8,128)S(1)}, f32[64,4,256]{2,0,1:T(8,128)S(1)}, u32[]{:S(2)}, u32[]{:S(2)}) collective-permute-start(f32[64,4,256]{2,0,1:T(8,128)S(1)} %slice.692), channel_id=1, source_target_pairs={{0,16},{4,20},{8,24},{12,28},{16,32},{20,36},{24,40},{28,44},{32,4... | collective-permute-start | bytes 786440 | tf_op jit(solution)/shard_map/ppermute | solution.py:12
  165.7 12.3 %all_gather.49 = f32[256,256]{1,0:T(8,128)S(1)} all-gather(f32[64,256]{1,0:T(8,128)S(1)} %fusion.88), channel_id=1, replica_groups=mesh['leaf'=128,'sep'=4] {'sep'}, dimensions={0}, use_global_device_ids=true | all-gather | bytes 327680 | tf_op jit(solution)/shard_map/all_gather | solution.py:34
  187.2 12.7 %collective-permute-done.8 = f32[64,3,256]{2,0,1:T(8,128)S(1)} collective-permute-done((f32[64,3,256]{2,0,1:T(8,128)S(1)}, f32[64,3,256]{2,0,1:T(8,128)S(1)}, u32[]{:S(2)}, u32[]{:S(2)}) %collective-permute-start.8) | collective-permute-done | bytes 196640 | tf_op jit(solution)/shard_map/ppermute | solution.py:12
  199.9 12.3 %all_gather.50 = f32[256,256]{1,0:T(8,128)S(1)} all-gather(f32[64,256]{1,0:T(8,128)S(1)} %fusion.86), channel_id=1, replica_groups=mesh['leaf'=128,'sep'=4] {'sep'}, dimensions={0}, use_global_device_ids=true | all-gather | bytes 327680 | tf_op jit(solution)/shard_map/all_gather | solution.py:34
  225.8 12.3 %all_gather.51 = f32[256,256]{1,0:T(8,128)S(1)} all-gather(f32[64,256]{1,0:T(8,128)S(1)} %fusion.85), channel_id=1, replica_groups=mesh['leaf'=128,'sep'=4] {'sep'}, dimensions={0}, use_global_device_ids=true | all-gather | bytes 327680 | tf_op jit(solution)/shard_map/all_gather | solution.py:34
  249.8 12.4 %all_gather.52 = f32[256,256]{1,0:T(8,128)S(1)} all-gather(f32[64,256]{1,0:T(8,128)S(1)} %bitcast_subtract_fusion), channel_id=1, replica_groups=mesh['leaf'=128,'sep'=4] {'sep'}, dimensions={0}, use_global_device_ids=true | all-gather | bytes 327680 | tf_op jit(solution)/shard_map/all_gather | solution.py:34
  275.3 12.7 %all-gather.1 = f32[256,1,256]{2,1,0:T(1,128)S(1)} all-gather(f32[64,1,256]{2,1,0:T(1,128)S(1)} %copy.70), channel_id=3, replica_groups=mesh['leaf'=128,'sep'=4] {'sep'}, dimensions={0}, use_global_device_ids=true | all-gather | bytes 327680 | tf_op jit(solution)/shard_map/all_gather | solution.py:34
  300.1 12.3 %all-gather.2 = f32[256,1,256]{2,1,0:T(1,128)S(1)} all-gather(f32[64,1,256]{2,1,0:T(1,128)S(1)} %copy.71), channel_id=4, replica_groups=mesh['leaf'=128,'sep'=4] {'sep'}, dimensions={0}, use_global_device_ids=true | all-gather | bytes 327680 | tf_op jit(solution)/shard_map/all_gather | solution.py:34
  313.6 6.9 %collective-permute-start.17 = (f32[64,3,256]{2,0,1:T(8,128)S(1)}, f32[64,3,256]{2,0,1:T(8,128)S(1)}, u32[]{:S(2)}, u32[]{:S(2)}) collective-permute-start(f32[64,3,256]{2,0,1:T(8,128)S(1)} %slice.705), channel_id=1, source_target_pairs={{0,32},{4,36},{8,40},{12,44},{16,48},{20,52},{24,56},{28,60},{32,6... | collective-permute-start | bytes 589832 | tf_op jit(solution)/shard_map/ppermute | solution.py:12
  324.8 12.8 %collective-permute-done.18 = f32[64,3,256]{2,0,1:T(8,128)S(1)} collective-permute-done((f32[64,3,256]{2,0,1:T(8,128)S(1)}, f32[64,3,256]{2,0,1:T(8,128)S(1)}, u32[]{:S(2)}, u32[]{:S(2)}) %collective-permute-start.18) | collective-permute-done | bytes 196640 | tf_op jit(solution)/shard_map/ppermute | solution.py:12
  337.7 12.8 %all-gather.3 = f32[256,1,256]{2,1,0:T(1,128)S(1)} all-gather(f32[64,1,256]{2,1,0:T(1,128)S(1)} %copy.72), channel_id=5, replica_groups=mesh['leaf'=128,'sep'=4] {'sep'}, dimensions={0}, use_global_device_ids=true | all-gather | bytes 327680 | tf_op jit(solution)/shard_map/all_gather | solution.py:34
  357.7 10.0 %collective-permute-done.20 = f32[64,4,256]{2,0,1:T(8,128)S(1)} collective-permute-done((f32[64,4,256]{2,0,1:T(8,128)S(1)}, f32[64,4,256]{2,0,1:T(8,128)S(1)}, u32[]{:S(2)}, u32[]{:S(2)}) %collective-permute-start.20) | collective-permute-done | bytes 262176 | tf_op jit(solution)/shard_map/ppermute | solution.py:12
  367.9 12.3 %all-gather.4 = f32[256,1,256]{2,1,0:T(1,128)S(1)} all-gather(f32[64,1,256]{2,1,0:T(1,128)S(1)} %copy.73), channel_id=6, replica_groups=mesh['leaf'=128,'sep'=4] {'sep'}, dimensions={0}, use_global_device_ids=true | all-gather | bytes 327680 | tf_op jit(solution)/shard_map/all_gather | solution.py:34
  396.6 12.3 %all-gather.5 = f32[256,1,256]{2,1,0:T(1,128)S(1)} all-gather(f32[64,1,256]{2,1,0:T(1,128)S(1)} %copy.74), channel_id=7, replica_groups=mesh['leaf'=128,'sep'=4] {'sep'}, dimensions={0}, use_global_device_ids=true | all-gather | bytes 327680 | tf_op jit(solution)/shard_map/all_gather | solution.py:34
  421.8 12.3 %all-gather.6 = f32[256,1,256]{2,1,0:T(1,128)S(1)} all-gather(f32[64,1,256]{2,1,0:T(1,128)S(1)} %copy.75), channel_id=8, replica_groups=mesh['leaf'=128,'sep'=4] {'sep'}, dimensions={0}, use_global_device_ids=true | all-gather | bytes 327680 | tf_op jit(solution)/shard_map/all_gather | solution.py:34
  437.3 6.0 %collective-permute-done.25 = f32[64,7,256]{2,0,1:T(8,128)S(1)} collective-permute-done((f32[64,7,256]{2,0,1:T(8,128)S(1)}, f32[64,7,256]{2,0,1:T(8,128)S(1)}, u32[]{:S(2)}, u32[]{:S(2)}) %collective-permute-start.25) | collective-permute-done | bytes 458784 | tf_op jit(solution)/shard_map/ppermute | solution.py:12
  444.5 32.9 %all-gather.9.cloned.1.call-done = f32[256,7,256]{2,0,1:T(8,128)} async-done(((f32[64,7,256]{2,0,1:T(8,128)}), f32[256,7,256]{2,0,1:T(8,128)}) %all-gather.9.cloned.1.call-update) | async-done | bytes 1835024 | tf_op jit(solution)/shard_map/all_gather | solution.py:34
  484.2 25.8 %reduce-scatter.7.cloned.1.call-done = f32[160,256]{1,0:T(8,128)} async-done(((f32[640,256]{1,0:T(8,128)}), f32[160,256]{1,0:T(8,128)}) %reduce-scatter.7.cloned.1.call-update) | async-done | bytes 163856
  (179 shorter events, 167.8 us)
Async XLA Ops:
  7.2 60.4 %reduce-scatter.5.cloned.1.call-start = ((), (), s32[]{:S(2)}) async-start(), calls=%async_computation.2 | async-start | bytes 2621440 | tf_op jit(solution)/shard_map/reduce_scatter | solution.py:73
  27.8 449.6 %all-gather.9.cloned.1.call-start = ((), (), s32[]{:S(2)}) async-start(), calls=%async_computation.3 | async-start | bytes 2293760 | tf_op jit(solution)/shard_map/all_gather | solution.py:34
  68.8 9.8 %collective-permute-start = (f32[64,7,256]{2,0,1:T(8,128)S(1)}, f32[64,7,256]{2,0,1:T(8,128)S(1)}, u32[]{:S(2)}, u32[]{:S(2)}) collective-permute-start(f32[64,7,256]{2,0,1:T(8,128)S(1)} %copy.67), channel_id=1, source_target_pairs={{0,4},{4,8},{8,12},{12,16},{16,20},{20,24},{24,28},{28,32},{32,36}... | collective-permute-start | bytes 1376264 | tf_op jit(solution)/shard_map/ppermute | solution.py:12
  93.2 9.1 %collective-permute-start.1 = (f32[64,6,256]{2,0,1:T(8,128)S(1)}, f32[64,6,256]{2,0,1:T(8,128)S(1)}, u32[]{:S(2)}, u32[]{:S(2)}) collective-permute-start(f32[64,6,256]{2,0,1:T(8,128)S(1)} %slice.686), channel_id=1, source_target_pairs={{0,4},{4,8},{8,12},{12,16},{16,20},{20,24},{24,28},{28,32},{32,36}... | collective-permute-start | bytes 1179656 | tf_op jit(solution)/shard_map/ppermute | solution.py:12
  95.2 8.9 %collective-permute-start.2 = (f32[64,6,256]{2,0,1:T(8,128)S(1)}, f32[64,6,256]{2,0,1:T(8,128)S(1)}, u32[]{:S(2)}, u32[]{:S(2)}) collective-permute-start(f32[64,6,256]{2,0,1:T(8,128)S(1)} %slice.686), channel_id=1, source_target_pairs={{4,0},{8,4},{12,8},{16,12},{20,16},{24,20},{28,24},{32,28},{36,32}... | collective-permute-start | bytes 1179656 | tf_op jit(solution)/shard_map/ppermute | solution.py:12
  117.8 10.7 %collective-permute-start.3 = (f32[64,5,256]{2,0,1:T(8,128)S(1)}, f32[64,5,256]{2,0,1:T(8,128)S(1)}, u32[]{:S(2)}, u32[]{:S(2)}) collective-permute-start(f32[64,5,256]{2,0,1:T(8,128)S(1)} %slice.689), channel_id=1, source_target_pairs={{0,8},{4,12},{8,16},{12,20},{16,24},{20,28},{24,32},{28,36},{32,40... | collective-permute-start | bytes 983048 | tf_op jit(solution)/shard_map/ppermute | solution.py:12
  121.2 11.9 %collective-permute-start.4 = (f32[64,5,256]{2,0,1:T(8,128)S(1)}, f32[64,5,256]{2,0,1:T(8,128)S(1)}, u32[]{:S(2)}, u32[]{:S(2)}) collective-permute-start(f32[64,5,256]{2,0,1:T(8,128)S(1)} %slice.689), channel_id=1, source_target_pairs={{8,0},{12,4},{16,8},{20,12},{24,16},{28,20},{32,24},{36,28},{40,32... | collective-permute-start | bytes 983048 | tf_op jit(solution)/shard_map/ppermute | solution.py:12
  146.5 12.8 %collective-permute-start.5 = (f32[64,4,256]{2,0,1:T(8,128)S(1)}, f32[64,4,256]{2,0,1:T(8,128)S(1)}, u32[]{:S(2)}, u32[]{:S(2)}) collective-permute-start(f32[64,4,256]{2,0,1:T(8,128)S(1)} %slice.692), channel_id=1, source_target_pairs={{0,16},{4,20},{8,24},{12,28},{16,32},{20,36},{24,40},{28,44},{32,4... | collective-permute-start | bytes 786440 | tf_op jit(solution)/shard_map/ppermute | solution.py:12
  152.7 12.0 %collective-permute-start.6 = (f32[64,4,256]{2,0,1:T(8,128)S(1)}, f32[64,4,256]{2,0,1:T(8,128)}, u32[]{:S(2)}, u32[]{:S(2)}) collective-permute-start(f32[64,4,256]{2,0,1:T(8,128)S(1)} %slice.692), channel_id=1, source_target_pairs={{16,0},{20,4},{24,8},{28,12},{32,16},{36,20},{40,24},{44,28},{48,3... | collective-permute-start | bytes 786440 | tf_op jit(solution)/shard_map/ppermute | solution.py:12
  178.9 8.2 %collective-permute-start.7 = (f32[64,3,256]{2,0,1:T(8,128)S(1)}, f32[64,3,256]{2,0,1:T(8,128)S(1)}, u32[]{:S(2)}, u32[]{:S(2)}) collective-permute-start(f32[64,3,256]{2,0,1:T(8,128)S(1)} %slice.695), channel_id=1, source_target_pairs={{0,32},{4,36},{8,40},{12,44},{16,48},{20,52},{24,56},{28,60},{32,6... | collective-permute-start | bytes 589832 | tf_op jit(solution)/shard_map/ppermute | solution.py:12
  182.6 17.3 %collective-permute-start.8 = (f32[64,3,256]{2,0,1:T(8,128)S(1)}, f32[64,3,256]{2,0,1:T(8,128)S(1)}, u32[]{:S(2)}, u32[]{:S(2)}) collective-permute-start(f32[64,3,256]{2,0,1:T(8,128)S(1)} %slice.695), channel_id=1, source_target_pairs={{32,0},{36,4},{40,8},{44,12},{48,16},{52,20},{56,24},{60,28},{64,3... | collective-permute-start | bytes 589832 | tf_op jit(solution)/shard_map/ppermute | solution.py:12
  213.2 7.0 %collective-permute-start.9 = (f32[64,2,256]{2,0,1:T(8,128)S(1)}, f32[64,2,256]{2,0,1:T(8,128)S(1)}, u32[]{:S(2)}, u32[]{:S(2)}) collective-permute-start(f32[64,2,256]{2,0,1:T(8,128)S(1)} %slice.698), channel_id=1, source_target_pairs={{0,64},{4,68},{8,72},{12,76},{16,80},{20,84},{24,88},{28,92},{32,9... | collective-permute-start | bytes 393224 | tf_op jit(solution)/shard_map/ppermute | solution.py:12
  217.7 7.2 %collective-permute-start.10 = (f32[64,2,256]{2,0,1:T(8,128)S(1)}, f32[64,2,256]{2,0,1:T(8,128)}, u32[]{:S(2)}, u32[]{:S(2)}) collective-permute-start(f32[64,2,256]{2,0,1:T(8,128)S(1)} %slice.698), channel_id=1, source_target_pairs={{64,0},{68,4},{72,8},{76,12},{80,16},{84,20},{88,24},{92,28},{96,3... | collective-permute-start | bytes 393224 | tf_op jit(solution)/shard_map/ppermute | solution.py:12
  242.7 7.1 %collective-permute-start.12 = (f32[64,1,256]{2,0,1:T(8,128)S(1)}, f32[64,1,256]{2,0,1:T(8,128)S(1)}, u32[]{:S(2)}, u32[]{:S(2)}) collective-permute-start(f32[64,1,256]{2,0,1:T(8,128)S(1)} %slice_add_fusion), channel_id=1, source_target_pairs={{128,0},{132,4},{136,8},{140,12},{144,16},{148,20},{152,24},{156,2... | collective-permute-start | bytes 196616 | tf_op jit(solution)/shard_map/ppermute | solution.py:12
  268.2 7.1 %collective-permute-start.14 = (f32[64,1,256]{2,0,1:T(8,128)S(1)}, f32[64,1,256]{2,0,1:T(8,128)S(1)}, u32[]{:S(2)}, u32[]{:S(2)}) collective-permute-start(f32[64,1,256]{2,0,1:T(8,128)S(1)} %select_bitcast_fusion), channel_id=1, source_target_pairs={{128,0},{132,4},{136,8},{140,12},{144,16},{148,20},{152,24},{156,2... | collective-permute-start | bytes 196616 | tf_op jit(solution)/shard_map/ppermute | solution.py:12
  313.6 11.1 %collective-permute-start.17 = (f32[64,3,256]{2,0,1:T(8,128)S(1)}, f32[64,3,256]{2,0,1:T(8,128)S(1)}, u32[]{:S(2)}, u32[]{:S(2)}) collective-permute-start(f32[64,3,256]{2,0,1:T(8,128)S(1)} %slice.705), channel_id=1, source_target_pairs={{0,32},{4,36},{8,40},{12,44},{16,48},{20,52},{24,56},{28,60},{32,6... | collective-permute-start | bytes 589832 | tf_op jit(solution)/shard_map/ppermute | solution.py:12
  320.6 17.0 %collective-permute-start.18 = (f32[64,3,256]{2,0,1:T(8,128)S(1)}, f32[64,3,256]{2,0,1:T(8,128)S(1)}, u32[]{:S(2)}, u32[]{:S(2)}) collective-permute-start(f32[64,3,256]{2,0,1:T(8,128)S(1)} %slice.705), channel_id=1, source_target_pairs={{32,0},{36,4},{40,8},{44,12},{48,16},{52,20},{56,24},{60,28},{64,3... | collective-permute-start | bytes 589832 | tf_op jit(solution)/shard_map/ppermute | solution.py:12
  353.8 13.9 %collective-permute-start.20 = (f32[64,4,256]{2,0,1:T(8,128)S(1)}, f32[64,4,256]{2,0,1:T(8,128)S(1)}, u32[]{:S(2)}, u32[]{:S(2)}) collective-permute-start(f32[64,4,256]{2,0,1:T(8,128)S(1)} %slice.708), channel_id=1, source_target_pairs={{16,0},{20,4},{24,8},{28,12},{32,16},{36,20},{40,24},{44,28},{48,3... | collective-permute-start | bytes 786440 | tf_op jit(solution)/shard_map/ppermute | solution.py:12
  382.1 9.0 %collective-permute-start.21 = (f32[64,5,256]{2,0,1:T(8,128)S(1)}, f32[64,5,256]{2,0,1:T(8,128)S(1)}, u32[]{:S(2)}, u32[]{:S(2)}) collective-permute-start(f32[64,5,256]{2,0,1:T(8,128)S(1)} %slice.711), channel_id=1, source_target_pairs={{0,8},{4,12},{8,16},{12,20},{16,24},{20,28},{24,32},{28,36},{32,40... | collective-permute-start | bytes 983048 | tf_op jit(solution)/shard_map/ppermute | solution.py:12
  386.0 10.3 %collective-permute-start.22 = (f32[64,5,256]{2,0,1:T(8,128)S(1)}, f32[64,5,256]{2,0,1:T(8,128)S(1)}, u32[]{:S(2)}, u32[]{:S(2)}) collective-permute-start(f32[64,5,256]{2,0,1:T(8,128)S(1)} %slice.711), channel_id=1, source_target_pairs={{8,0},{12,4},{16,8},{20,12},{24,16},{28,20},{32,24},{36,28},{40,32... | collective-permute-start | bytes 983048 | tf_op jit(solution)/shard_map/ppermute | solution.py:12
  410.7 9.1 %collective-permute-start.23 = (f32[64,6,256]{2,0,1:T(8,128)S(1)}, f32[64,6,256]{2,0,1:T(8,128)S(1)}, u32[]{:S(2)}, u32[]{:S(2)}) collective-permute-start(f32[64,6,256]{2,0,1:T(8,128)S(1)} %slice.714), channel_id=1, source_target_pairs={{0,4},{4,8},{8,12},{12,16},{16,20},{20,24},{24,28},{28,32},{32,36}... | collective-permute-start | bytes 1179656 | tf_op jit(solution)/shard_map/ppermute | solution.py:12
  412.6 8.9 %collective-permute-start.24 = (f32[64,6,256]{2,0,1:T(8,128)S(1)}, f32[64,6,256]{2,0,1:T(8,128)S(1)}, u32[]{:S(2)}, u32[]{:S(2)}) collective-permute-start(f32[64,6,256]{2,0,1:T(8,128)S(1)} %slice.714), channel_id=1, source_target_pairs={{4,0},{8,4},{12,8},{16,12},{20,16},{24,20},{28,24},{32,28},{36,32}... | collective-permute-start | bytes 1179656 | tf_op jit(solution)/shard_map/ppermute | solution.py:12
  435.4 7.9 %collective-permute-start.25 = (f32[64,7,256]{2,0,1:T(8,128)S(1)}, f32[64,7,256]{2,0,1:T(8,128)S(1)}, u32[]{:S(2)}, u32[]{:S(2)}) collective-permute-start(f32[64,7,256]{2,0,1:T(8,128)S(1)} %get-tuple-element.328), channel_id=1, source_target_pairs={{4,0},{8,4},{12,8},{16,12},{20,16},{24,20},{28,24},{32,28},{36,32}... | collective-permute-start | bytes 1376264 | tf_op jit(solution)/shard_map/ppermute | solution.py:12
  444.2 65.8 %reduce-scatter.7.cloned.1.call-start = ((), (), s32[]{:S(2)}) async-start(), calls=%async_computation.4 | async-start | bytes 819200
  (17 other events, 327.0 us)
Sparse Core Ops, SparseCore 0:
  27.9 39.6 reduce-scatter.4
  444.3 33.0 all-gather.8
  482.7 27.2 reduce-scatter.6
where the time goes:
time: 519 us; the launch traced here: 518 us
  waiting for transfers between devices  218 us (42%)
  blocking collectives  175 us (34%)
  starting transfers between devices  72.1 us (14%)
  matrix products  21.9 us (4%)
  between operations  15 us (3%)
  local copies, waits for them, and re-layouts  8.57 us (2%)
  other arithmetic  7.86 us (2%)
    all_gather x13, blocking collectives, sep_rows(): return lax.all_gather(payload, 'sep', axis=0, tiled=True)  161 us
    ppermute x26, waiting for transfers between devices, passed_along(): return lax.ppermute(x, axis, pairs)  120 us
    ppermute x26, starting transfers between devices, passed_along(): return lax.ppermute(x, axis, pairs)  71.8 us
    reduce_scatter x1, waiting for transfers between devices, per_device(): lax.psum_scatter(densified, 'sep', scatter_dimension=0, tiled=True)  39.7 us
    all_gather x1, waiting for transfers between devices, sep_rows(): return lax.all_gather(payload, 'sep', axis=0, tiled=True)  32.9 us
    unnamed x4, waiting for transfers between devices  25.8 us
    all_gather x1, blocking collectives, per_device(): lax.all_gather(source, 'sep', axis=0, tiled=True)  13.7 us
  transfers between devices with their start and end apart: 29, of which 29 were waited for; matrix products, arithmetic and copies ran while one was open for 0% of the time, Pallas kernels for 0%

commit v1 on v0

--- a/solution.py
+++ b/solution.py
@@ -31,7 +31,9 @@
 
 
 def sep_rows(payload):
-    return lax.all_gather(payload, "sep", axis=0, tiled=True)
+    return jnp.concatenate(
+        lax.all_to_all(jnp.stack([payload] * lax.axis_size("sep")), "sep", 0, 0), axis=0
+    )
 
 
 def per_device(

time: 519 us -> 483 us (0.931)
  blocking collectives: 175 us -> 87 us
  starting transfers between devices: 72.1 us -> 105 us
  waiting for transfers between devices: 218 us -> 230 us
  local copies, waits for them, and re-layouts: 8.57 us -> 14.5 us
    all_gather x13 -> x0, blocking collectives: 161 us -> none  [sep_rows(): return lax.all_gather(payload, 'sep', axis=0, tiled=True)]
    all_to_all x0 -> x8, blocking collectives: none -> 73.2 us  [sep_rows(): lax.all_to_all(jnp.stack([payload] * lax.axis_size('sep')), 'sep', 0, 0)]
    all_to_all x0 -> x6, waiting for transfers between devices: none -> 58.4 us  [sep_rows(): lax.all_to_all(jnp.stack([payload] * lax.axis_size('sep')), 'sep', 0, 0)]
    all_gather x1 -> x0, waiting for transfers between devices: 32.9 us -> none  [sep_rows(): return lax.all_gather(payload, 'sep', axis=0, tiled=True)]
    all_to_all x0 -> x6, starting transfers between devices: none -> 20.7 us  [sep_rows(): lax.all_to_all(jnp.stack([payload] * lax.axis_size('sep')), 'sep', 0, 0)]
    ppermute x26, starting transfers between devices: 71.8 us -> 84.1 us  [passed_along(): return lax.ppermute(x, axis, pairs)]
    ppermute x26, waiting for transfers between devices: 120 us -> 110 us  [passed_along(): return lax.ppermute(x, axis, pairs)]
    another operation x0 -> x19, local copies, waits for them, and re-layouts: none -> 5.27 us  [sep_rows(): jnp.stack([payload] * lax.axis_size('sep'))]
  transfers between devices with their start and end apart: 29 -> 34, of which waited for: 29 -> 34; matrix products, arithmetic and copies ran while one was open for 0% -> 0% of each run, Pallas kernels for 0% -> 0%
where the time goes in v1:
time: 483 us; the launch traced here: 481 us
  waiting for transfers between devices  230 us (48%)
  starting transfers between devices  105 us (22%)
  blocking collectives  87 us (18%)
  matrix products  22.5 us (5%)
  between operations  15.4 us (3%)
  local copies, waits for them, and re-layouts  14.5 us (3%)
  other arithmetic  7.11 us (1%)
    ppermute x26, waiting for transfers between devices, passed_along(): return lax.ppermute(x, axis, pairs)  110 us
    ppermute x26, starting transfers between devices, passed_along(): return lax.ppermute(x, axis, pairs)  84.1 us
    all_to_all x8, blocking collectives, sep_rows(): lax.all_to_all(jnp.stack([payload] * lax.axis_size('sep')), 'sep', 0, 0)  73.2 us
    all_to_all x6, waiting for transfers between devices, sep_rows(): lax.all_to_all(jnp.stack([payload] * lax.axis_size('sep')), 'sep', 0, 0)  58.4 us
    reduce_scatter x1, waiting for transfers between devices, per_device(): lax.psum_scatter(densified, 'sep', scatter_dimension=0, tiled=True)  39.8 us
    unnamed x3, waiting for transfers between devices  21.1 us
    all_to_all x6, starting transfers between devices, sep_rows(): lax.all_to_all(jnp.stack([payload] * lax.axis_size('sep')), 'sep', 0, 0)  20.7 us
    all_gather x1, blocking collectives, per_device(): lax.all_gather(source, 'sep', axis=0, tiled=True)  13.7 us
  transfers between devices with their start and end apart: 34, of which 34 were waited for; matrix products, arithmetic and copies ran while one was open for 0% of the time, Pallas kernels for 0%

profile of v1, /device:TPU:8, one launch (start us, length us, event | category | flops | bytes accessed | tf_op | source)
XLA Modules:
  0.0 481.3 jit_solution(7659402302962781347)
XLA Ops:
  7.2 13.7 %all-gather = f32[1,640,256]{2,1,0:T(8,128)S(1)} all-gather(f32[1,160,256]{2,1,0:T(8,128)} %param.62), channel_id=2, replica_groups=mesh['leaf'=128,'sep'=4] {'sep'}, dimensions={1}, use_global_device_ids=true | all-gather | bytes 819200 | tf_op jit(solution)/shard_map/all_gather | solution.py:61
  29.9 39.8 %reduce-scatter.5.cloned.1.call-done = f32[64,7,256]{2,1,0:T(8,128)} async-done(((f32[256,7,256]{2,1,0:T(8,128)}), f32[64,7,256]{2,1,0:T(8,128)}) %reduce-scatter.5.cloned.1.call-update) | async-done | bytes 458768 | tf_op jit(solution)/shard_map/reduce_scatter | solution.py:75
  73.0 7.9 %collective-permute-done = f32[64,7,256]{2,0,1:T(8,128)S(1)} collective-permute-done((f32[64,7,256]{2,0,1:T(8,128)S(1)}, f32[64,7,256]{2,0,1:T(8,128)S(1)}, u32[]{:S(2)}, u32[]{:S(2)}) %collective-permute-start) | collective-permute-done | bytes 458784 | tf_op jit(solution)/shard_map/ppermute | solution.py:12
  86.2 6.6 %all-to-all-done = f32[4,64,256]{2,1,0:T(8,128)S(1)} async-done(((f32[4,64,256]{2,1,0:T(8,128)}), f32[4,64,256]{2,1,0:T(8,128)S(1)}, u32[]{:S(2)}, u32[]{:S(2)}) %all-to-all-start) | async-done | bytes 262176 | tf_op jit(solution)/shard_map/all_to_all | solution.py:35
  109.0 7.3 %all-to-all-done.1 = f32[4,64,256]{2,1,0:T(8,128)S(1)} async-done(((f32[4,64,256]{2,1,0:T(8,128)}), f32[4,64,256]{2,1,0:T(8,128)S(1)}, u32[]{:S(2)}, u32[]{:S(2)}) %all-to-all-start.1) | async-done | bytes 262176 | tf_op jit(solution)/shard_map/all_to_all | solution.py:35
  134.8 7.0 %all-to-all-done.2 = f32[4,64,256]{2,1,0:T(8,128)S(1)} async-done(((f32[4,64,256]{2,1,0:T(8,128)}), f32[4,64,256]{2,1,0:T(8,128)S(1)}, u32[]{:S(2)}, u32[]{:S(2)}) %all-to-all-start.2) | async-done | bytes 262176 | tf_op jit(solution)/shard_map/all_to_all | solution.py:35
  142.8 8.9 %collective-permute-start.5 = (f32[64,4,256]{2,0,1:T(8,128)S(1)}, f32[64,4,256]{2,0,1:T(8,128)S(1)}, u32[]{:S(2)}, u32[]{:S(2)}) collective-permute-start(f32[64,4,256]{2,0,1:T(8,128)S(1)} %slice.692), channel_id=1, source_target_pairs={{0,16},{4,20},{8,24},{12,28},{16,32},{20,36},{24,40},{28,44},{32,4... | collective-permute-start | bytes 786440 | tf_op jit(solution)/shard_map/ppermute | solution.py:12
  156.8 7.0 %collective-permute-done.6 = f32[64,4,256]{2,0,1:T(8,128)} collective-permute-done((f32[64,4,256]{2,0,1:T(8,128)S(1)}, f32[64,4,256]{2,0,1:T(8,128)}, u32[]{:S(2)}, u32[]{:S(2)}) %collective-permute-start.6) | collective-permute-done | bytes 262176 | tf_op jit(solution)/shard_map/ppermute | solution.py:12
  176.6 6.9 %collective-permute-start.7 = (f32[64,3,256]{2,0,1:T(8,128)S(1)}, f32[64,3,256]{2,0,1:T(8,128)S(1)}, u32[]{:S(2)}, u32[]{:S(2)}) collective-permute-start(f32[64,3,256]{2,0,1:T(8,128)S(1)} %slice.695), channel_id=1, source_target_pairs={{0,32},{4,36},{8,40},{12,44},{16,48},{20,52},{24,56},{28,60},{32,6... | collective-permute-start | bytes 589832 | tf_op jit(solution)/shard_map/ppermute | solution.py:12
  186.7 14.5 %collective-permute-done.8 = f32[64,3,256]{2,0,1:T(8,128)} collective-permute-done((f32[64,3,256]{2,0,1:T(8,128)S(1)}, f32[64,3,256]{2,0,1:T(8,128)}, u32[]{:S(2)}, u32[]{:S(2)}) %collective-permute-start.8) | collective-permute-done | bytes 196640 | tf_op jit(solution)/shard_map/ppermute | solution.py:12
  222.4 9.1 %all_to_all.70 = f32[4,64,256]{2,1,0:T(8,128)S(1)} all-to-all(f32[4,64,256]{2,1,0:T(8,128)S(1)} %stack.99), channel_id=1, replica_groups=mesh['leaf'=128,'sep'=4] {'sep'}, dimensions={0} | all-to-all | bytes 524288 | tf_op jit(solution)/shard_map/all_to_all | solution.py:35
  240.1 8.5 %collective-permute-done.12 = f32[64,1,256]{2,0,1:T(8,128)S(1)} collective-permute-done((f32[64,1,256]{2,0,1:T(8,128)S(1)}, f32[64,1,256]{2,0,1:T(8,128)S(1)}, u32[]{:S(2)}, u32[]{:S(2)}) %collective-permute-start.12) | collective-permute-done | bytes 65568 | tf_op jit(solution)/shard_map/ppermute | solution.py:12
  248.7 9.1 %all_to_all.71 = f32[4,64,256]{2,1,0:T(8,128)S(1)} all-to-all(f32[4,64,256]{2,1,0:T(8,128)S(1)} %stack.101), channel_id=1, replica_groups=mesh['leaf'=128,'sep'=4] {'sep'}, dimensions={0} | all-to-all | bytes 524288 | tf_op jit(solution)/shard_map/all_to_all | solution.py:35
  272.1 9.1 %all_to_all.72 = f32[4,64,256]{2,1,0:T(8,128)S(1)} all-to-all(f32[4,64,256]{2,1,0:T(8,128)S(1)} %stack.102), channel_id=1, replica_groups=mesh['leaf'=128,'sep'=4] {'sep'}, dimensions={0} | all-to-all | bytes 524288 | tf_op jit(solution)/shard_map/all_to_all | solution.py:35
  291.1 9.1 %all_to_all.73 = f32[4,64,256]{2,1,0:T(8,128)S(1)} all-to-all(f32[4,64,256]{2,1,0:T(8,128)S(1)} %stack.103), channel_id=1, replica_groups=mesh['leaf'=128,'sep'=4] {'sep'}, dimensions={0} | all-to-all | bytes 524288 | tf_op jit(solution)/shard_map/all_to_all | solution.py:35
  301.4 7.1 %collective-permute-start.17 = (f32[64,3,256]{2,0,1:T(8,128)S(1)}, f32[64,3,256]{2,0,1:T(8,128)S(1)}, u32[]{:S(2)}, u32[]{:S(2)}) collective-permute-start(f32[64,3,256]{2,0,1:T(8,128)S(1)} %slice.705), channel_id=1, source_target_pairs={{0,32},{4,36},{8,40},{12,44},{16,48},{20,52},{24,56},{28,60},{32,6... | collective-permute-start | bytes 589832 | tf_op jit(solution)/shard_map/ppermute | solution.py:12
  312.2 10.6 %collective-permute-done.18 = f32[64,3,256]{2,0,1:T(8,128)S(1)} collective-permute-done((f32[64,3,256]{2,0,1:T(8,128)S(1)}, f32[64,3,256]{2,0,1:T(8,128)S(1)}, u32[]{:S(2)}, u32[]{:S(2)}) %collective-permute-start.18) | collective-permute-done | bytes 196640 | tf_op jit(solution)/shard_map/ppermute | solution.py:12
  322.9 9.1 %all_to_all.74 = f32[4,64,256]{2,1,0:T(8,128)S(1)} all-to-all(f32[4,64,256]{2,1,0:T(8,128)S(1)} %stack.104), channel_id=1, replica_groups=mesh['leaf'=128,'sep'=4] {'sep'}, dimensions={0} | all-to-all | bytes 524288 | tf_op jit(solution)/shard_map/all_to_all | solution.py:35
  345.2 9.1 %all_to_all.75 = f32[4,64,256]{2,1,0:T(8,128)S(1)} all-to-all(f32[4,64,256]{2,1,0:T(8,128)S(1)} %stack.105), channel_id=1, replica_groups=mesh['leaf'=128,'sep'=4] {'sep'}, dimensions={0} | all-to-all | bytes 524288 | tf_op jit(solution)/shard_map/all_to_all | solution.py:35
  356.1 8.9 %collective-permute-start.21 = (f32[64,5,256]{2,0,1:T(8,128)S(1)}, f32[64,5,256]{2,0,1:T(8,128)S(1)}, u32[]{:S(2)}, u32[]{:S(2)}) collective-permute-start(f32[64,5,256]{2,0,1:T(8,128)S(1)} %slice.711), channel_id=1, source_target_pairs={{0,8},{4,12},{8,16},{12,20},{16,24},{20,28},{24,32},{28,36},{32,40... | collective-permute-start | bytes 983048 | tf_op jit(solution)/shard_map/ppermute | solution.py:12
  374.2 9.1 %all_to_all.76 = f32[4,64,256]{2,1,0:T(8,128)S(1)} all-to-all(f32[4,64,256]{2,1,0:T(8,128)S(1)} %stack.106), channel_id=1, replica_groups=mesh['leaf'=128,'sep'=4] {'sep'}, dimensions={0} | all-to-all | bytes 524288 | tf_op jit(solution)/shard_map/all_to_all | solution.py:35
  396.3 9.8 %all_to_all.77 = f32[4,64,256]{2,1,0:T(8,128)S(1)} all-to-all(f32[4,64,256]{2,1,0:T(8,128)S(1)} %stack.107), channel_id=1, replica_groups=mesh['leaf'=128,'sep'=4] {'sep'}, dimensions={0} | all-to-all | bytes 524288 | tf_op jit(solution)/shard_map/all_to_all | solution.py:35
  420.9 24.3 %all-to-all-done.13 = f32[4,64,7,256]{3,1,2,0:T(8,128)S(1)} async-done(((f32[4,64,7,256]{3,1,2,0:T(8,128)}), f32[4,64,7,256]{3,1,2,0:T(8,128)S(1)}, u32[]{:S(2)}, u32[]{:S(2)}) %all-to-all-start.13) | async-done | bytes 1835040 | tf_op jit(solution)/shard_map/all_to_all | solution.py:35
  451.5 21.1 %reduce-scatter.7.cloned.1.call-done = f32[160,256]{1,0:T(8,128)} async-done(((f32[640,256]{1,0:T(8,128)}), f32[160,256]{1,0:T(8,128)}) %reduce-scatter.7.cloned.1.call-update) | async-done | bytes 163856
  (192 shorter events, 192.7 us)
Async XLA Ops:
  7.2 62.5 %reduce-scatter.5.cloned.1.call-start = ((), (), s32[]{:S(2)}) async-start(), calls=%async_computation.16 | async-start | bytes 2621440 | tf_op jit(solution)/shard_map/reduce_scatter | solution.py:75
  70.9 9.9 %collective-permute-start = (f32[64,7,256]{2,0,1:T(8,128)S(1)}, f32[64,7,256]{2,0,1:T(8,128)S(1)}, u32[]{:S(2)}, u32[]{:S(2)}) collective-permute-start(f32[64,7,256]{2,0,1:T(8,128)S(1)} %copy.105), channel_id=1, source_target_pairs={{0,4},{4,8},{8,12},{12,16},{16,20},{20,24},{24,28},{28,32},{32,36}... | collective-permute-start | bytes 1376264 | tf_op jit(solution)/shard_map/ppermute | solution.py:12
  82.8 10.1 %all-to-all-start = ((f32[4,64,256]{2,1,0:T(8,128)}), f32[4,64,256]{2,1,0:T(8,128)S(1)}, u32[]{:S(2)}, u32[]{:S(2)}) async-start(f32[4,64,256]{2,1,0:T(8,128)} %stack.43), calls=%async_computation.1 | async-start | bytes 524288 | tf_op jit(solution)/shard_map/all_to_all | solution.py:35
  93.9 9.1 %collective-permute-start.1 = (f32[64,6,256]{2,0,1:T(8,128)S(1)}, f32[64,6,256]{2,0,1:T(8,128)S(1)}, u32[]{:S(2)}, u32[]{:S(2)}) collective-permute-start(f32[64,6,256]{2,0,1:T(8,128)S(1)} %slice.686), channel_id=1, source_target_pairs={{0,4},{4,8},{8,12},{12,16},{16,20},{20,24},{24,28},{28,32},{32,36}... | collective-permute-start | bytes 1179656 | tf_op jit(solution)/shard_map/ppermute | solution.py:12
  95.8 8.9 %collective-permute-start.2 = (f32[64,6,256]{2,0,1:T(8,128)S(1)}, f32[64,6,256]{2,0,1:T(8,128)S(1)}, u32[]{:S(2)}, u32[]{:S(2)}) collective-permute-start(f32[64,6,256]{2,0,1:T(8,128)S(1)} %slice.686), channel_id=1, source_target_pairs={{4,0},{8,4},{12,8},{16,12},{20,16},{24,20},{28,24},{32,28},{36,32}... | collective-permute-start | bytes 1179656 | tf_op jit(solution)/shard_map/ppermute | solution.py:12
  105.6 10.7 %all-to-all-start.1 = ((f32[4,64,256]{2,1,0:T(8,128)}), f32[4,64,256]{2,1,0:T(8,128)S(1)}, u32[]{:S(2)}, u32[]{:S(2)}) async-start(f32[4,64,256]{2,1,0:T(8,128)} %stack.45), calls=%async_computation.2 | async-start | bytes 524288 | tf_op jit(solution)/shard_map/all_to_all | solution.py:35
  117.3 12.1 %collective-permute-start.3 = (f32[64,5,256]{2,0,1:T(8,128)S(1)}, f32[64,5,256]{2,0,1:T(8,128)S(1)}, u32[]{:S(2)}, u32[]{:S(2)}) collective-permute-start(f32[64,5,256]{2,0,1:T(8,128)S(1)} %slice.689), channel_id=1, source_target_pairs={{0,8},{4,12},{8,16},{12,20},{16,24},{20,28},{24,32},{28,36},{32,40... | collective-permute-start | bytes 983048 | tf_op jit(solution)/shard_map/ppermute | solution.py:12
  120.1 10.5 %collective-permute-start.4 = (f32[64,5,256]{2,0,1:T(8,128)S(1)}, f32[64,5,256]{2,0,1:T(8,128)S(1)}, u32[]{:S(2)}, u32[]{:S(2)}) collective-permute-start(f32[64,5,256]{2,0,1:T(8,128)S(1)} %slice.689), channel_id=1, source_target_pairs={{8,0},{12,4},{16,8},{20,12},{24,16},{28,20},{32,24},{36,28},{40,32... | collective-permute-start | bytes 983048 | tf_op jit(solution)/shard_map/ppermute | solution.py:12
  131.4 10.4 %all-to-all-start.2 = ((f32[4,64,256]{2,1,0:T(8,128)}), f32[4,64,256]{2,1,0:T(8,128)S(1)}, u32[]{:S(2)}, u32[]{:S(2)}) async-start(f32[4,64,256]{2,1,0:T(8,128)} %stack.93), calls=%async_computation.3 | async-start | bytes 524288 | tf_op jit(solution)/shard_map/all_to_all | solution.py:35
  142.8 14.0 %collective-permute-start.5 = (f32[64,4,256]{2,0,1:T(8,128)S(1)}, f32[64,4,256]{2,0,1:T(8,128)S(1)}, u32[]{:S(2)}, u32[]{:S(2)}) collective-permute-start(f32[64,4,256]{2,0,1:T(8,128)S(1)} %slice.692), channel_id=1, source_target_pairs={{0,16},{4,20},{8,24},{12,28},{16,32},{20,36},{24,40},{28,44},{32,4... | collective-permute-start | bytes 786440 | tf_op jit(solution)/shard_map/ppermute | solution.py:12
  151.7 12.1 %collective-permute-start.6 = (f32[64,4,256]{2,0,1:T(8,128)S(1)}, f32[64,4,256]{2,0,1:T(8,128)}, u32[]{:S(2)}, u32[]{:S(2)}) collective-permute-start(f32[64,4,256]{2,0,1:T(8,128)S(1)} %slice.692), channel_id=1, source_target_pairs={{16,0},{20,4},{24,8},{28,12},{32,16},{36,20},{40,24},{44,28},{48,3... | collective-permute-start | bytes 786440 | tf_op jit(solution)/shard_map/ppermute | solution.py:12
  165.5 10.1 %all-to-all-start.3 = ((f32[4,64,256]{2,1,0:T(8,128)}), f32[4,64,256]{2,1,0:T(8,128)S(1)}, u32[]{:S(2)}, u32[]{:S(2)}) async-start(f32[4,64,256]{2,1,0:T(8,128)} %stack.95), calls=%async_computation.4 | async-start | bytes 524288 | tf_op jit(solution)/shard_map/all_to_all | solution.py:35
  176.6 10.2 %collective-permute-start.7 = (f32[64,3,256]{2,0,1:T(8,128)S(1)}, f32[64,3,256]{2,0,1:T(8,128)S(1)}, u32[]{:S(2)}, u32[]{:S(2)}) collective-permute-start(f32[64,3,256]{2,0,1:T(8,128)S(1)} %slice.695), channel_id=1, source_target_pairs={{0,32},{4,36},{8,40},{12,44},{16,48},{20,52},{24,56},{28,60},{32,6... | collective-permute-start | bytes 589832 | tf_op jit(solution)/shard_map/ppermute | solution.py:12
  183.5 17.7 %collective-permute-start.8 = (f32[64,3,256]{2,0,1:T(8,128)S(1)}, f32[64,3,256]{2,0,1:T(8,128)}, u32[]{:S(2)}, u32[]{:S(2)}) collective-permute-start(f32[64,3,256]{2,0,1:T(8,128)S(1)} %slice.695), channel_id=1, source_target_pairs={{32,0},{36,4},{40,8},{44,12},{48,16},{52,20},{56,24},{60,28},{64,3... | collective-permute-start | bytes 589832 | tf_op jit(solution)/shard_map/ppermute | solution.py:12
  202.9 10.1 %all-to-all-start.4 = ((f32[4,64,256]{2,1,0:T(8,128)}), f32[4,64,256]{2,1,0:T(8,128)S(1)}, u32[]{:S(2)}, u32[]{:S(2)}) async-start(f32[4,64,256]{2,1,0:T(8,128)} %stack.97), calls=%async_computation.5 | async-start | bytes 524288 | tf_op jit(solution)/shard_map/all_to_all | solution.py:35
  238.3 10.4 %collective-permute-start.12 = (f32[64,1,256]{2,0,1:T(8,128)S(1)}, f32[64,1,256]{2,0,1:T(8,128)S(1)}, u32[]{:S(2)}, u32[]{:S(2)}) collective-permute-start(f32[64,1,256]{2,0,1:T(8,128)S(1)} %slice_add_fusion), channel_id=1, source_target_pairs={{128,0},{132,4},{136,8},{140,12},{144,16},{148,20},{152,24},{156,2... | collective-permute-start | bytes 196616 | tf_op jit(solution)/shard_map/ppermute | solution.py:12
  301.4 10.8 %collective-permute-start.17 = (f32[64,3,256]{2,0,1:T(8,128)S(1)}, f32[64,3,256]{2,0,1:T(8,128)S(1)}, u32[]{:S(2)}, u32[]{:S(2)}) collective-permute-start(f32[64,3,256]{2,0,1:T(8,128)S(1)} %slice.705), channel_id=1, source_target_pairs={{0,32},{4,36},{8,40},{12,44},{16,48},{20,52},{24,56},{28,60},{32,6... | collective-permute-start | bytes 589832 | tf_op jit(solution)/shard_map/ppermute | solution.py:12
  308.5 14.3 %collective-permute-start.18 = (f32[64,3,256]{2,0,1:T(8,128)S(1)}, f32[64,3,256]{2,0,1:T(8,128)S(1)}, u32[]{:S(2)}, u32[]{:S(2)}) collective-permute-start(f32[64,3,256]{2,0,1:T(8,128)S(1)} %slice.705), channel_id=1, source_target_pairs={{32,0},{36,4},{40,8},{44,12},{48,16},{52,20},{56,24},{60,28},{64,3... | collective-permute-start | bytes 589832 | tf_op jit(solution)/shard_map/ppermute | solution.py:12
  335.2 9.8 %collective-permute-start.20 = (f32[64,4,256]{2,0,1:T(8,128)S(1)}, f32[64,4,256]{2,0,1:T(8,128)S(1)}, u32[]{:S(2)}, u32[]{:S(2)}) collective-permute-start(f32[64,4,256]{2,0,1:T(8,128)S(1)} %slice.708), channel_id=1, source_target_pairs={{16,0},{20,4},{24,8},{28,12},{32,16},{36,20},{40,24},{44,28},{48,3... | collective-permute-start | bytes 786440 | tf_op jit(solution)/shard_map/ppermute | solution.py:12
  356.1 13.5 %collective-permute-start.21 = (f32[64,5,256]{2,0,1:T(8,128)S(1)}, f32[64,5,256]{2,0,1:T(8,128)S(1)}, u32[]{:S(2)}, u32[]{:S(2)}) collective-permute-start(f32[64,5,256]{2,0,1:T(8,128)S(1)} %slice.711), channel_id=1, source_target_pairs={{0,8},{4,12},{8,16},{12,20},{16,24},{20,28},{24,32},{28,36},{32,40... | collective-permute-start | bytes 983048 | tf_op jit(solution)/shard_map/ppermute | solution.py:12
  365.1 9.0 %collective-permute-start.22 = (f32[64,5,256]{2,0,1:T(8,128)S(1)}, f32[64,5,256]{2,0,1:T(8,128)S(1)}, u32[]{:S(2)}, u32[]{:S(2)}) collective-permute-start(f32[64,5,256]{2,0,1:T(8,128)S(1)} %slice.711), channel_id=1, source_target_pairs={{8,0},{12,4},{16,8},{20,12},{24,16},{28,20},{32,24},{36,28},{40,32... | collective-permute-start | bytes 983048 | tf_op jit(solution)/shard_map/ppermute | solution.py:12
  385.2 9.1 %collective-permute-start.23 = (f32[64,6,256]{2,0,1:T(8,128)S(1)}, f32[64,6,256]{2,0,1:T(8,128)S(1)}, u32[]{:S(2)}, u32[]{:S(2)}) collective-permute-start(f32[64,6,256]{2,0,1:T(8,128)S(1)} %slice.714), channel_id=1, source_target_pairs={{0,4},{4,8},{8,12},{12,16},{16,20},{20,24},{24,28},{28,32},{32,36}... | collective-permute-start | bytes 1179656 | tf_op jit(solution)/shard_map/ppermute | solution.py:12
  416.8 28.4 %all-to-all-start.13 = ((f32[4,64,7,256]{3,1,2,0:T(8,128)}), f32[4,64,7,256]{3,1,2,0:T(8,128)S(1)}, u32[]{:S(2)}, u32[]{:S(2)}) async-start(f32[4,64,7,256]{3,1,2,0:T(8,128)} %stack.108), calls=%async_computation.14 | async-start | bytes 3670016 | tf_op jit(solution)/shard_map/all_to_all | solution.py:35
  420.5 52.1 %reduce-scatter.7.cloned.1.call-start = ((), (), s32[]{:S(2)}) async-start(), calls=%async_computation.17 | async-start | bytes 819200
  (22 other events, 265.9 us)
Sparse Core Ops, SparseCore 0:
  30.0 39.6 reduce-scatter.4
  450.0 22.5 reduce-scatter.6
